TPU v7x, 512 devices: a whole 4x4x16 slice. The times are simulated.
512 devices in a mesh: ctx: 64 (over x, z), head: 8 (over y, core).
Axes of the slice: x: 4, y: 4, z: 16, core: 2. Of those that a mesh axis runs over, the one named last changes fastest.
Arguments:
- lin_query: bfloat16 [16384, 4096], P('ctx', 'head'), may hold values from -200 to 200
- lin_keys: bfloat16 [16384, 4096], P('ctx', 'head'), may hold values from -6 to 6
- lin_values: bfloat16 [16384, 4096], P('ctx', 'head'), may hold values from -6 to 6
- lin_grad: bfloat16 [16384, 4096], P('ctx', 'head'), may hold values from -6 to 6
- norm_gain: float32 [4096], P('head'), may hold values from 0.1 to 1.9
- log_decay: float32 [32, 16384], P('head'), may hold values from -1 to 0, as said below
- state_in: bfloat16 [64, 32, 128, 128], P('ctx', 'head'), may hold values from -96 to 96
- soft_query: bfloat16 [16384, 8192], P('ctx', 'head'), may hold values from -10 to 10
- soft_keys: bfloat16 [16384, 1024], P('ctx', 'head'), may hold values from -4 to 4
- soft_values: bfloat16 [16384, 1024], P('ctx', 'head'), may hold values from -6 to 6
- soft_grad: bfloat16 [16384, 8192], P('ctx', 'head'), may hold values from -6 to 6
- projections: bfloat16 [2, 4096, 1024], P(None, None, 'head'), may hold values from -0.125 to 0.125
- doc_lengths: int32 [32], replicated, may hold values from 1 to 768, 16384 in all
Outputs:
- lin_dq: bfloat16 [16384, 4096], P('ctx', 'head')
- lin_dk: bfloat16 [16384, 4096], P('ctx', 'head')
- lin_dv: bfloat16 [16384, 4096], P('ctx', 'head')
- soft_dq: bfloat16 [16384, 8192], P('ctx', 'head')
- soft_dk: bfloat16 [16384, 1024], P('ctx', 'head')
- soft_dv: bfloat16 [16384, 1024], P('ctx', 'head')
Inputs may be any that keep to these rules, and one draw needn't show every extreme that they name: `log_decay`: strictly negative. `doc_lengths`: positive lengths that add up to 16384; the largest is exactly 768.
All inputs are finite; a program needn't handle non-finite values.
Results may differ from a plain program's by a relative error of at most 0.011.
Values may be sent and summed in bfloat16 or wider, within the bound.
No kernel may reach another device: no remote copies, remote signals or barrier semaphores. Data moves between devices by JAX's collectives and lax.ppermute only.
A program may use at most 128 MiB of HBM per device.

v0:
```python
import jax
import jax.numpy as jnp
from jax import lax
from jax.sharding import PartitionSpec as P

DH = 128
Q_HEADS = 64
KV_HEADS = 8
LIGHTNING_HEADS = 32
SUB = 4
epsilon = 1e-06
precise = lax.Precision.HIGHEST


def passed_along(block, axis, distance):
    devices = range(lax.axis_size(axis))
    route = [(i - distance, i) for i in devices if i - distance in devices]
    return lax.ppermute(block, axis, route)


def document_of(positions, doc_lengths):
    doc_ends = jnp.cumsum(doc_lengths)
    return jnp.sum((doc_ends[None, :] <= positions[:, None]).astype(jnp.int32), axis=1)


def decay_weights(log_block):
    running = jnp.cumsum(log_block, axis=1)
    position = jnp.arange(log_block.shape[1], dtype=jnp.int32)
    before = position[:, None] >= position[None, :]
    log_gap = running[:, :, None] - running[:, None, :]
    weights = jnp.where(before[None], jnp.exp(jnp.minimum(log_gap, 0.0)), 0.0)
    return (running, weights)


def lightning_part(lin_query, lin_keys, lin_values, cotangent, norm_gain, log_decay, state_in):
    length = lin_query.shape[0]
    head_count = lin_query.shape[1] // DH
    device = lax.axis_index("ctx")
    chain = lax.axis_size("ctx")
    log_block = lax.dynamic_slice_in_dim(log_decay, device * length, length, 1)
    running, weights = decay_weights(log_block)
    query_blk = lin_query.reshape(length, head_count, DH)
    key_blk = lin_keys.reshape(length, head_count, DH)
    value_blk = lin_values.reshape(length, head_count, DH)
    grad_blk = cotangent.reshape(length, head_count, DH)
    state_blk = state_in[0]
    near_terms = (
        jnp.einsum("thd,shd->hts", query_blk, key_blk, preferred_element_type=jnp.float32) * weights
    ).astype(jnp.bfloat16)
    growth = jnp.exp(running).T[:, :, None]
    scaled = (query_blk.astype(jnp.float32) * growth).astype(jnp.bfloat16)
    inside = jnp.einsum("hts,shd->thd", near_terms, value_blk, preferred_element_type=jnp.float32)
    carried = jnp.einsum("thd,hde->the", scaled, state_blk, preferred_element_type=jnp.float32)
    lin_out = (inside + carried) / DH
    gated = norm_gain.reshape(head_count, DH)[None] * grad_blk
    squares, cross_term = lax.psum(
        (jnp.sum(lin_out * lin_out, axis=(1, 2)), jnp.sum(gated * lin_out, axis=(1, 2))), "head"
    )
    features = LIGHTNING_HEADS * DH
    spread = jnp.sqrt(squares / features + epsilon)
    out_grad = (
        gated / spread[:, None, None]
        - lin_out * (cross_term / (features * spread**3))[:, None, None]
    ).astype(jnp.bfloat16)
    far_terms = (
        jnp.einsum("the,she->hts", out_grad, value_blk, preferred_element_type=jnp.float32)
        * weights
    ).astype(jnp.bfloat16)
    grad_query = (
        jnp.einsum("hts,shd->thd", far_terms, key_blk, preferred_element_type=jnp.float32)
        + growth
        * jnp.einsum("the,hde->thd", out_grad, state_blk, preferred_element_type=jnp.float32)
    ) / DH
    summary = jnp.einsum(
        "thd,the->hde", scaled, out_grad, preferred_element_type=jnp.float32
    ).astype(jnp.bfloat16)
    own_total = running[:, -1]
    totals = jnp.sum(log_decay.reshape(head_count, chain, length), axis=2)
    starts = jnp.concatenate(
        [jnp.zeros((head_count, 1), jnp.float32), jnp.cumsum(totals, axis=1)], axis=1
    )
    anchor = lax.dynamic_slice_in_dim(starts, device + 1, 1, 1)
    block_in = lax.all_gather(summary[None], "ctx", axis=0, tiled=True)
    block_count = block_in.shape[0]
    block_index = jnp.arange(block_count, dtype=jnp.int32)
    log_level = lax.slice_in_dim(starts, 0, block_count, axis=1)
    factors = jnp.where(
        block_index[None, :] > device, jnp.exp(jnp.minimum(log_level - anchor, 0.0)), 0.0
    )
    after_state = jnp.einsum(
        "hn,nhde->hde", factors, block_in.astype(jnp.float32), precision=precise
    )
    after_low = after_state.astype(jnp.bfloat16)
    tail_decay = jnp.exp(own_total[:, None] - running).T[:, :, None]
    grad_key = (
        jnp.einsum("hst,shd->thd", far_terms, query_blk, preferred_element_type=jnp.float32)
        + tail_decay
        * jnp.einsum("the,hde->thd", value_blk, after_low, preferred_element_type=jnp.float32)
    ) / DH
    grad_value = (
        jnp.einsum("hst,she->the", near_terms, out_grad, preferred_element_type=jnp.float32)
        + tail_decay
        * jnp.einsum("thd,hde->the", key_blk, after_low, preferred_element_type=jnp.float32)
    ) / DH
    flat = (length, head_count * DH)
    return (
        grad_query.astype(jnp.bfloat16).reshape(flat),
        grad_key.astype(jnp.bfloat16).reshape(flat),
        grad_value.astype(jnp.bfloat16).reshape(flat),
    )


def softmax_head(query_heads, grad_heads, key_win, value_win, visible):
    head_count, length, features = query_heads.shape
    per_turn = min(head_count, max(1, 512 // length))
    turn_count = head_count // per_turn
    query_steps = query_heads.reshape(turn_count, per_turn * length, features)
    grad_steps = grad_heads.reshape(turn_count, per_turn * length, features)
    visible_rows = jnp.tile(visible, (per_turn, 1))
    score_scale = DH ** (-0.5)
    contract_last = (((1,), (1,)), ((), ()))
    contract_first = (((0,), (0,)), ((), ()))

    def one_turn(running_sums, pieces):
        query_rows, grad_rows = pieces
        scores = (
            lax.dot_general(query_rows, key_win, contract_last, preferred_element_type=jnp.float32)
            * score_scale
        )
        scores = jnp.where(visible_rows, scores, -1e30)
        highest = jnp.max(scores, axis=1, keepdims=True)
        raised = jnp.where(visible_rows, jnp.exp(scores - highest), 0.0)
        attention = raised / jnp.sum(raised, axis=1, keepdims=True)
        prob_low = attention.astype(jnp.bfloat16)
        output = jnp.dot(prob_low, value_win, preferred_element_type=jnp.float32)
        row_delta = jnp.sum(grad_rows.astype(jnp.float32) * output, axis=1, keepdims=True)
        grad_probs = lax.dot_general(
            grad_rows, value_win, contract_last, preferred_element_type=jnp.float32
        )
        dscore = (attention * (grad_probs - row_delta) * score_scale).astype(jnp.bfloat16)
        grad_query = jnp.dot(dscore, key_win, preferred_element_type=jnp.float32).astype(
            jnp.bfloat16
        )
        part_key = lax.dot_general(
            dscore, query_rows, contract_first, preferred_element_type=jnp.float32
        )
        part_value = lax.dot_general(
            prob_low, grad_rows, contract_first, preferred_element_type=jnp.float32
        )
        return ((running_sums[0] + part_key, running_sums[1] + part_value), grad_query)

    zero_rows = jnp.zeros((key_win.shape[0], features), jnp.float32)
    sums_out, grad_query = lax.scan(one_turn, (zero_rows, zero_rows), (query_steps, grad_steps))
    return (sums_out[0], sums_out[1], grad_query.reshape(head_count, length, features))


def softmax_part(soft_query, soft_keys, soft_values, soft_grad, doc_lengths):
    length = soft_query.shape[0]
    kv_local = soft_keys.shape[1] // DH
    group_size = Q_HEADS // KV_HEADS
    device = lax.axis_index("ctx")
    stacked = jnp.stack([soft_keys, soft_values])
    arrived = [stacked] + [passed_along(stacked, "ctx", offset) for offset in range(1, SUB)]
    window = jnp.concatenate(arrived[::-1], axis=1)
    query_pos = device * length + jnp.arange(length, dtype=jnp.int32)
    key_pos = (device - (SUB - 1)) * length + jnp.arange(SUB * length, dtype=jnp.int32)
    visible = (
        (key_pos[None, :] <= query_pos[:, None])
        & (key_pos[None, :] >= 0)
        & (
            document_of(key_pos, doc_lengths)[None, :]
            == document_of(query_pos, doc_lengths)[:, None]
        )
    )
    query_split = soft_query.reshape(length, kv_local, group_size, DH)
    grad_split = soft_grad.reshape(length, kv_local, group_size, DH)
    key_win = window[0, :, 0:DH]
    value_win = window[1, :, 0:DH]
    query_heads = jnp.transpose(query_split[:, 0], (1, 0, 2))
    grad_heads = jnp.transpose(grad_split[:, 0], (1, 0, 2))
    grad_key, grad_value, grad_query = softmax_head(
        query_heads, grad_heads, key_win, value_win, visible
    )
    query_grads = [jnp.transpose(grad_query, (1, 0, 2))]
    soft_dq = jnp.stack(query_grads, axis=1).reshape(length, kv_local * group_size * DH)
    partial_value = jnp.stack([grad_key, grad_value])

    def block_of(offset):
        slot = SUB - 1 - offset
        return partial_value[:, slot * length : (slot + 1) * length]

    summed = block_of(0)
    for offset in range(1, SUB):
        summed = summed + passed_along(block_of(offset), "ctx", -offset)
    return (soft_dq, summed[0].astype(jnp.bfloat16), summed[1].astype(jnp.bfloat16))


def per_device(
    lin_query,
    lin_keys,
    lin_values,
    lin_grad,
    norm_gain,
    log_decay,
    state_in,
    soft_query,
    soft_keys,
    soft_values,
    soft_grad,
    projections,
    doc_lengths,
):
    soft_dq, soft_dk, soft_dv = softmax_part(
        soft_query, soft_keys, soft_values, soft_grad, doc_lengths
    )
    kv_grads = jnp.stack([soft_dk, soft_dv], axis=1)
    carried_back = lax.psum_scatter(
        jnp.einsum("crk,tck->rt", projections, kv_grads, preferred_element_type=jnp.float32),
        "head",
        scatter_dimension=0,
        tiled=True,
    )
    cotangent = lin_grad.astype(jnp.float32) + carried_back.T
    lin_dq, lin_dk, lin_dv = lightning_part(
        lin_query, lin_keys, lin_values, cotangent, norm_gain, log_decay, state_in
    )
    return (lin_dq, lin_dk, lin_dv, soft_dq, soft_dk, soft_dv)


def solution(mesh):
    in_specs = (
        P("ctx", "head"),
        P("ctx", "head"),
        P("ctx", "head"),
        P("ctx", "head"),
        P("head"),
        P("head", None),
        P("ctx", "head", None, None),
        P("ctx", "head"),
        P("ctx", "head"),
        P("ctx", "head"),
        P("ctx", "head"),
        P(None, None, "head"),
        P(),
    )
    out_specs = (
        P("ctx", "head"),
        P("ctx", "head"),
        P("ctx", "head"),
        P("ctx", "head"),
        P("ctx", "head"),
        P("ctx", "head"),
    )
    return jax.shard_map(
        per_device, mesh=mesh, in_specs=in_specs, out_specs=out_specs, check_vma=False
    )
```

profile of v0, /device:TPU:32, one launch (start us, length us, event | category | flops | bytes accessed | tf_op | source)
XLA Modules:
  0.0 368.0 jit_solution(18281954963981145327)
XLA Ops:
  8.3 3.8 %collective-permute-start.2 = (bf16[2,256,128]{2,1,0:T(8,128)(2,1)S(1)}, bf16[2,256,128]{2,1,0:T(8,128)(2,1)S(1)}, u32[]{:S(2)}, u32[]{:S(2)}) collective-permute-start(bf16[2,256,128]{2,1,0:T(8,128)(2,1)S(1)} %pad_maximum_fusion.1), channel_id=1, source_target_pairs={{0,8},{8,16},{16,24},{24,32},{32,40},{40,48},{48,56},{56,64},{64,7... | collective-permute-start | bytes 393224 | tf_op jit(solution)/shard_map/ppermute | solution.py:18
  12.1 7.0 %collective-permute-start.1 = (bf16[2,256,128]{2,1,0:T(8,128)(2,1)S(1)}, bf16[2,256,128]{2,1,0:T(8,128)(2,1)}, u32[]{:S(2)}, u32[]{:S(2)}) collective-permute-start(bf16[2,256,128]{2,1,0:T(8,128)(2,1)S(1)} %pad_maximum_fusion.1), channel_id=1, source_target_pairs={{0,16},{8,24},{16,32},{24,40},{32,48},{40,56},{48,64},{56,72},{64,... | collective-permute-start | bytes 393224 | tf_op jit(solution)/shard_map/ppermute | solution.py:18
  19.2 6.5 %collective-permute-start = (bf16[2,256,128]{2,1,0:T(8,128)(2,1)S(1)}, bf16[2,256,128]{2,1,0:T(8,128)(2,1)}, u32[]{:S(2)}, u32[]{:S(2)}) collective-permute-start(bf16[2,256,128]{2,1,0:T(8,128)(2,1)S(1)} %pad_maximum_fusion.1), channel_id=1, source_target_pairs={{0,24},{8,32},{16,40},{24,48},{32,56},{40,64},{48,72},{56,80},{64,... | collective-permute-start | bytes 393224 | tf_op jit(solution)/shard_map/ppermute | solution.py:18
  27.4 1.9 copy_bitcast_fusion.1
  29.3 1.2 copy.123
  33.8 39.3 %while.15 = (s32[]{:T(128)}, f32[1024,128]{1,0:T(8,128)}, f32[1024,128]{1,0:T(8,128)S(1)}, bf16[4,512,128]{2,1,0:T(8,128)(2,1)}, bf16[4,512,128]{2,1,0:T(8,128)(...) while((s32[]{:T(128)}, f32[1024,128]{1,0:T(8,128)}, ...), condition=%wide.region_7.8_spmd.clone, body=%wide.region_3.7_spmd.clone.sunk | while | flops 816052736 | bytes 27801824 | solution.py:153
  35.5 1.5 fusion.122
  41.0 1.5 convolution_add_fusion.5
  45.4 1.5 fusion.122
  50.9 1.5 convolution_add_fusion.5
  55.2 1.5 fusion.122
  60.7 1.5 convolution_add_fusion.5
  65.0 1.5 fusion.122
  70.5 1.5 convolution_add_fusion.5
  74.3 1.9 collective-permute-start.3
  76.2 1.3 collective-permute-start.5
  77.5 1.3 collective-permute-start.4
  78.8 10.3 %collective-permute-done.3 = f32[2,256,128]{2,1,0:T(8,128)S(1)} collective-permute-done((f32[2,256,128]{2,1,0:T(8,128)S(1)}, f32[2,256,128]{2,1,0:T(8,128)S(1)}, u32[]{:S(2)}, u32[]{:S(2)}) %collective-permute-start.3) | collective-permute-done | bytes 262176 | tf_op jit(solution)/shard_map/ppermute | solution.py:18
  89.1 19.3 %collective-permute-done.5 = f32[2,256,128]{2,1,0:T(8,128)S(1)} collective-permute-done((f32[2,256,128]{2,1,0:T(8,128)S(1)}, f32[2,256,128]{2,1,0:T(8,128)S(1)}, u32[]{:S(2)}, u32[]{:S(2)}) %collective-permute-start.5) | collective-permute-done | bytes 262176 | tf_op jit(solution)/shard_map/ppermute | solution.py:18
  108.5 4.6 %collective-permute-done.4 = f32[2,256,128]{2,1,0:T(8,128)S(1)} collective-permute-done((f32[2,256,128]{2,1,0:T(8,128)S(1)}, f32[2,256,128]{2,1,0:T(8,128)S(1)}, u32[]{:S(2)}, u32[]{:S(2)}) %collective-permute-start.4) | collective-permute-done | bytes 262176 | tf_op jit(solution)/shard_map/ppermute | solution.py:18
  113.8 2.7 convolution_bitcast_fusion
  122.3 42.6 %reduce-scatter.2.cloned.1.call-done = f32[512,256]{0,1:T(8,128)} async-done(((f32[4096,256]{0,1:T(8,128)}), f32[512,256]{0,1:T(8,128)}) %reduce-scatter.2.cloned.1.call-update) | async-done | bytes 524304 | tf_op jit(solution)/shard_map/reduce_scatter | solution.py:217
  164.9 1.9 bitcast_add_fusion
  168.1 2.2 fusion.36
  170.3 13.1 %all-reduce.1 = (f32[256]{0:T(256)S(1)}, f32[256]{0:T(256)S(1)}) all-reduce(f32[256]{0:T(256)S(1)} %get-tuple-element.158, f32[256]{0:T(256)S(1)} %get-tuple-element.157), channel_id=1, replica_groups=mesh['ctx'=64,'head'=8] {'head'}, use_global_device_ids=true, to_apply=%region_14.15 | all-reduce | flops 512 | bytes 4096 | tf_op jit(solution)/shard_map/psum | solution.py:56
  187.1 1.4 copy.145
  189.4 1.5 fusion.22
  194.2 1.3 convolution_bitcast_fusion.1
  195.5 146.7 %all-gather.3.cloned.1.call-done = bf16[256,128,128]{2,1,0:T(8,128)(2,1)} async-done(((bf16[4,128,128]{2,1,0:T(8,128)(2,1)}), bf16[256,128,128]{2,1,0:T(8,128)(2,1)}) %all-gather.3.cloned.1.call-update) | async-done | bytes 8388624 | tf_op jit(solution)/shard_map/all_gather | solution.py:83
  342.2 12.2 %fusion.19 = bf16[4,1,128,128]{3,1,2,0:T(2,128)(2,1)} fusion(f32[4,64,1,1]{1,2,3,0:T(1,128)S(1)} %bitcast.267, bf16[64,4,128,128]{3,2,1,0:T(8,128)(2,1)} %bitcast.244), kind=kOutput, calls=%fused_computation.26 | convolution fusion | flops 50331648 | bytes 8520704 | tf_op jit(solution)/shard_map/hn,nhde->hde/dot_general | solution.py:90
  355.4 1.9 fusion.33
  357.3 1.8 copy.148
  (146 shorter events, 52.9 us)
Async XLA Ops:
  7.2 106.6 %copy-start = (bf16[2,4096,128]{2,1,0:T(8,128)(2,1)S(1)}, bf16[2,4096,128]{2,1,0:T(8,128)(2,1)}, u32[]{:S(2)}) copy-start(bf16[2,4096,128]{2,1,0:T(8,128)(2,1)} %param.26) | copy-start | bytes 6291460
  7.2 25.6 %copy-start.14 = (bf16[256,128]{1,0:T(8,128)(2,1)S(1)}, bf16[256,128]{1,0:T(8,128)(2,1)}, u32[]{:S(2)}) copy-start(bf16[256,128]{1,0:T(8,128)(2,1)} %param.24) | copy-start | bytes 196612
  7.2 25.6 %copy-start.15 = (bf16[256,128]{1,0:T(8,128)(2,1)S(1)}, bf16[256,128]{1,0:T(8,128)(2,1)}, u32[]{:S(2)}) copy-start(bf16[256,128]{1,0:T(8,128)(2,1)} %param.23) | copy-start | bytes 196612
  7.2 157.7 %reduce-scatter.2.cloned.1.call-start = ((), (), s32[]{:S(2)}) async-start(), calls=%async_computation.1 | async-start | bytes 4718592 | tf_op jit(solution)/shard_map/reduce_scatter | solution.py:217
  8.3 24.3 %collective-permute-start.2 = (bf16[2,256,128]{2,1,0:T(8,128)(2,1)S(1)}, bf16[2,256,128]{2,1,0:T(8,128)(2,1)S(1)}, u32[]{:S(2)}, u32[]{:S(2)}) collective-permute-start(bf16[2,256,128]{2,1,0:T(8,128)(2,1)S(1)} %pad_maximum_fusion.1), channel_id=1, source_target_pairs={{0,8},{8,16},{16,24},{24,32},{32,40},{40,48},{48,56},{56,64},{64,7... | collective-permute-start | bytes 393224 | tf_op jit(solution)/shard_map/ppermute | solution.py:18
  12.1 20.5 %collective-permute-start.1 = (bf16[2,256,128]{2,1,0:T(8,128)(2,1)S(1)}, bf16[2,256,128]{2,1,0:T(8,128)(2,1)}, u32[]{:S(2)}, u32[]{:S(2)}) collective-permute-start(bf16[2,256,128]{2,1,0:T(8,128)(2,1)S(1)} %pad_maximum_fusion.1), channel_id=1, source_target_pairs={{0,16},{8,24},{16,32},{24,40},{32,48},{40,56},{48,64},{56,72},{64,... | collective-permute-start | bytes 393224 | tf_op jit(solution)/shard_map/ppermute | solution.py:18
  19.2 13.6 %collective-permute-start = (bf16[2,256,128]{2,1,0:T(8,128)(2,1)S(1)}, bf16[2,256,128]{2,1,0:T(8,128)(2,1)}, u32[]{:S(2)}, u32[]{:S(2)}) collective-permute-start(bf16[2,256,128]{2,1,0:T(8,128)(2,1)S(1)} %pad_maximum_fusion.1), channel_id=1, source_target_pairs={{0,24},{8,32},{16,40},{24,48},{32,56},{40,64},{48,72},{56,80},{64,... | collective-permute-start | bytes 393224 | tf_op jit(solution)/shard_map/ppermute | solution.py:18
  37.9 0.9 copy-start.4
  40.0 1.0 copy-start.1
  42.5 1.1 copy-start.2
  47.7 0.9 copy-start.4
  49.8 1.0 copy-start.1
  52.4 1.1 copy-start.2
  57.5 0.9 copy-start.4
  59.6 1.0 copy-start.1
  62.2 1.1 copy-start.2
  67.4 0.9 copy-start.4
  69.4 1.0 copy-start.1
  72.0 1.1 copy-start.2
  73.1 39.9 %copy-start.3 = (f32[1024,128]{1,0:T(8,128)S(1)}, f32[1024,128]{1,0:T(8,128)}, u32[]{:S(2)}) copy-start(f32[1024,128]{1,0:T(8,128)} %get-tuple-element.55) | copy-start | bytes 1572868
  74.3 14.9 %collective-permute-start.3 = (f32[2,256,128]{2,1,0:T(8,128)S(1)}, f32[2,256,128]{2,1,0:T(8,128)S(1)}, u32[]{:S(2)}, u32[]{:S(2)}) collective-permute-start(f32[2,256,128]{2,1,0:T(8,128)S(1)} %get-tuple-element.181), channel_id=1, source_target_pairs={{8,0},{16,8},{24,16},{32,24},{40,32},{48,40},{56,48},{64,56},{72,6... | collective-permute-start | bytes 786440 | tf_op jit(solution)/shard_map/ppermute | solution.py:18
  76.2 32.3 %collective-permute-start.5 = (f32[2,256,128]{2,1,0:T(8,128)S(1)}, f32[2,256,128]{2,1,0:T(8,128)S(1)}, u32[]{:S(2)}, u32[]{:S(2)}) collective-permute-start(f32[2,256,128]{2,1,0:T(8,128)S(1)} %get-tuple-element.182), channel_id=1, source_target_pairs={{24,0},{32,8},{40,16},{48,24},{56,32},{64,40},{72,48},{80,56},{88,... | collective-permute-start | bytes 786440 | tf_op jit(solution)/shard_map/ppermute | solution.py:18
  77.5 35.5 %collective-permute-start.4 = (f32[2,256,128]{2,1,0:T(8,128)S(1)}, f32[2,256,128]{2,1,0:T(8,128)S(1)}, u32[]{:S(2)}, u32[]{:S(2)}) collective-permute-start(f32[2,256,128]{2,1,0:T(8,128)S(1)} %get-tuple-element.183), channel_id=1, source_target_pairs={{16,0},{24,8},{32,16},{40,24},{48,32},{56,40},{64,48},{72,56},{80,... | collective-permute-start | bytes 786440 | tf_op jit(solution)/shard_map/ppermute | solution.py:18
  116.4 2.6 copy-start.13
  116.5 3.4 copy-start.9
  116.5 4.7 %copy-start.10 = (bf16[256,512]{1,0:T(8,128)(2,1)S(1)}, bf16[256,512]{1,0:T(8,128)(2,1)}, u32[]{:S(2)}) copy-start(bf16[256,512]{1,0:T(8,128)(2,1)} %param.17) | copy-start | bytes 786436
  116.5 225.7 %all-gather.3.cloned.1.call-start = ((), (), s32[]{:S(2)}) async-start(), calls=%async_computation.2 | async-start | bytes 8519680 | tf_op jit(solution)/shard_map/all_gather | solution.py:83
  118.6 46.3 %copy-start.12 = (bf16[256,512]{1,0:T(8,128)(2,1)S(1)}, bf16[256,512]{1,0:T(8,128)(2,1)}, u32[]{:S(2)}) copy-start(bf16[256,512]{1,0:T(8,128)(2,1)} %param.18) | copy-start | bytes 786436
  121.2 46.9 %copy-start.11 = (bf16[1,4,128,128]{3,2,1,0:T(8,128)(2,1)S(1)}, bf16[1,4,128,128]{3,2,1,0:T(8,128)(2,1)}, u32[]{:S(2)}) copy-start(bf16[1,4,128,128]{3,2,1,0:T(8,128)(2,1)} %param.21) | copy-start | bytes 393220
  121.2 46.9 %copy-start.17 = (f32[512]{0:T(512)S(1)}, f32[512]{0:T(512)}, u32[]{:S(2)}) copy-start(f32[512]{0:T(512)} %param.19) | copy-start | bytes 6148
  189.4 3.7 %copy-start.6 = (bf16[4,256,256]{2,1,0:T(8,128)(2,1)S(1)}, bf16[4,256,256]{2,1,0:T(8,128)(2,1)}, u32[]{:S(2)}) copy-start(bf16[4,256,256]{2,1,0:T(8,128)(2,1)} %copy-done.5) | copy-start | bytes 1572868
  342.2 13.3 %copy-start.7 = (f32[256,4,128]{0,2,1:T(8,128)S(1)}, f32[256,4,128]{0,2,1:T(8,128)}, u32[]{:S(2)}) copy-start(f32[256,4,128]{0,2,1:T(8,128)} %convolution_bitcast_fusion.4) | copy-start | bytes 1572868
  (3 other events, 2.3 us)
Sparse Core Ops, SparseCore 0:
  116.6 48.2 reduce-scatter.1
  185.7 156.4 all-gather.2
where the time goes:
time: 369 us; the launch traced here: 368 us
  waiting for transfers between devices  224 us (61%)
  matrix products  49.9 us (14%)
  local copies, waits for them, and re-layouts  27.2 us (7%)
  starting transfers between devices  22 us (6%)
  other arithmetic  17.5 us (5%)
  between operations  14.3 us (4%)
  blocking collectives  13.1 us (4%)
    all_gather x1, waiting for transfers between devices, lightning_part(): block_in = lax.all_gather(summary[None], 'ctx', axis=0, tiled=True)  147 us
    reduce_scatter x1, waiting for transfers between devices, per_device(): lax.psum_scatter(jnp.einsum('crk,tck->rt', projections, kv_grads, preferr...  42.6 us
    ppermute x6, waiting for transfers between devices, passed_along(): return lax.ppermute(block, axis, route)  34.4 us
    ppermute x6, starting transfers between devices, passed_along(): return lax.ppermute(block, axis, route)  21.9 us
    psum x1, blocking collectives, lightning_part(): lax.psum((jnp.sum(lin_out * lin_out, axis=(1, 2)), jnp.sum(gated * lin_ou...  13.1 us
    dot_general x1, matrix products, lightning_part(): jnp.einsum('hn,nhde->hde', factors, block_in.astype(jnp.float32), precisi...  12.2 us
    unnamed x38, local copies, waits for them, and re-layouts  8.16 us
  transfers between devices with their start and end apart: 8, of which 6 were waited for; matrix products, arithmetic and copies ran while one was open for 6% of the time, Pallas kernels for 0%

commit v1 on v0

--- a/solution.py
+++ b/solution.py
@@ -10,6 +10,13 @@
 SUB = 4
 epsilon = 1e-06
 precise = lax.Precision.HIGHEST
+
+
+def gather_over(shard, mesh_axis, dim):
+    size = lax.axis_size(mesh_axis)
+    shards = jnp.stack([shard for _ in range(size)])
+    shards = lax.all_to_all(shards, mesh_axis, split_axis=0, concat_axis=0)
+    return jnp.concatenate(shards, axis=dim)
 
 
 def passed_along(block, axis, distance):
@@ -80,7 +87,7 @@
         [jnp.zeros((head_count, 1), jnp.float32), jnp.cumsum(totals, axis=1)], axis=1
     )
     anchor = lax.dynamic_slice_in_dim(starts, device + 1, 1, 1)
-    block_in = lax.all_gather(summary[None], "ctx", axis=0, tiled=True)
+    block_in = gather_over(summary[None], "ctx", 0)
     block_count = block_in.shape[0]
     block_index = jnp.arange(block_count, dtype=jnp.int32)
     log_level = lax.slice_in_dim(starts, 0, block_count, axis=1)

time: 369 us -> 617 us (1.67)
  waiting for transfers between devices: 224 us -> 436 us
  matrix products: 49.9 us -> 67.3 us
  starting transfers between devices: 22 us -> 37.3 us
  other arithmetic: 17.5 us -> 25.1 us
    all_to_all x0 -> x1, waiting for transfers between devices: none -> 358 us  [gather_over(): shards = lax.all_to_all(shards, mesh_axis, split_axis=0, concat_axis=0)]
    all_gather x1 -> x0, waiting for transfers between devices: 147 us -> none  [lightning_part(): block_in = lax.all_gather(summary[None], 'ctx', axis=0, tiled=True)]
    all_to_all x0 -> x1, starting transfers between devices: none -> 16 us  [gather_over(): shards = lax.all_to_all(shards, mesh_axis, split_axis=0, concat_axis=0)]
    dot_general x4, matrix products: 2.03 us -> 8.91 us  [one_turn(): output = jnp.dot(prob_low, value_win, preferred_element_type=jnp.float32)]
  transfers between devices with their start and end apart: 8 -> 8, of which waited for: 6 -> 6; matrix products, arithmetic and copies ran while one was open for 6% -> 3% of each run, Pallas kernels for 0% -> 0%
where the time goes in v1:
time: 617 us; the launch traced here: 615 us
  waiting for transfers between devices  436 us (71%)
  matrix products  67.3 us (11%)
  starting transfers between devices  37.3 us (6%)
  other arithmetic  25.1 us (4%)
  local copies, waits for them, and re-layouts  21.8 us (4%)
  between operations  14.4 us (2%)
  blocking collectives  13 us (2%)
    all_to_all x1, waiting for transfers between devices, gather_over(): shards = lax.all_to_all(shards, mesh_axis, split_axis=0, concat_axis=0)  358 us
    reduce_scatter x1, waiting for transfers between devices, per_device(): lax.psum_scatter(jnp.einsum('crk,tck->rt', projections, kv_grads, preferr...  40.2 us
    ppermute x6, waiting for transfers between devices, passed_along(): return lax.ppermute(block, axis, route)  38.4 us
    ppermute x6, starting transfers between devices, passed_along(): return lax.ppermute(block, axis, route)  21.3 us
    all_to_all x1, starting transfers between devices, gather_over(): shards = lax.all_to_all(shards, mesh_axis, split_axis=0, concat_axis=0)  16 us
    psum x1, blocking collectives, lightning_part(): lax.psum((jnp.sum(lin_out * lin_out, axis=(1, 2)), jnp.sum(gated * lin_ou...  13 us
  transfers between devices with their start and end apart: 8, of which 6 were waited for; matrix products, arithmetic and copies ran while one was open for 3% of the time, Pallas kernels for 0%

profile of v1, /device:TPU:32, one launch (start us, length us, event | category | flops | bytes accessed | tf_op | source)
XLA Modules:
  0.0 615.5 jit_solution(14931589498535866414)
XLA Ops:
  8.3 7.7 %collective-permute-start = (bf16[2,256,128]{2,1,0:T(8,128)(2,1)S(1)}, bf16[2,256,128]{2,1,0:T(8,128)(2,1)S(1)}, u32[]{:S(2)}, u32[]{:S(2)}) collective-permute-start(bf16[2,256,128]{2,1,0:T(8,128)(2,1)S(1)} %pad_maximum_fusion.1), channel_id=1, source_target_pairs={{0,24},{8,32},{16,40},{24,48},{32,56},{40,64},{48,72},{56,80},{64,... | collective-permute-start | bytes 393224 | tf_op jit(solution)/shard_map/ppermute | solution.py:25
  16.0 5.8 collective-permute-start.1
  21.9 3.2 collective-permute-start.2
  31.2 3.3 collective-permute-done.2
  35.6 60.0 %while.15 = (s32[]{:T(128)}, f32[1024,128]{1,0:T(8,128)}, f32[1024,128]{1,0:T(8,128)}, bf16[4,512,128]{2,1,0:T(8,128)(2,1)}, bf16[4,512,128]{2,1,0:T(8,128)(2,1)...) while((s32[]{:T(128)}, f32[1024,128]{1,0:T(8,128)}, ...), condition=%wide.region_7.8_spmd.clone, body=%wide.region_3.7_spmd.clone.sunk | while | flops 816052736 | bytes 48250204 | solution.py:160
  37.1 2.1 fusion.124
  40.3 2.2 fusion.125
  43.9 2.3 convolution_add_fusion.5
  51.1 2.1 fusion.124
  54.3 2.2 fusion.125
  57.9 2.5 convolution_add_fusion.5
  62.5 2.4 convolution_add_fusion.6
  66.4 2.1 fusion.124
  69.6 2.2 fusion.125
  73.3 2.5 convolution_add_fusion.5
  75.8 2.1 fusion.126
  77.8 2.4 convolution_add_fusion.6
  81.8 2.1 fusion.124
  84.9 2.2 fusion.125
  88.6 2.5 convolution_add_fusion.5
  93.2 2.4 convolution_add_fusion.6
  101.4 10.9 %collective-permute-done.3 = f32[2,256,128]{2,1,0:T(8,128)S(1)} collective-permute-done((f32[2,256,128]{2,1,0:T(8,128)S(1)}, f32[2,256,128]{2,1,0:T(8,128)S(1)}, u32[]{:S(2)}, u32[]{:S(2)}) %collective-permute-start.3) | collective-permute-done | bytes 262176 | tf_op jit(solution)/shard_map/ppermute | solution.py:25
  112.4 3.4 collective-permute-done.4
  115.8 20.7 %collective-permute-done.5 = f32[2,256,128]{2,1,0:T(8,128)S(1)} collective-permute-done((f32[2,256,128]{2,1,0:T(8,128)S(1)}, f32[2,256,128]{2,1,0:T(8,128)S(1)}, u32[]{:S(2)}, u32[]{:S(2)}) %collective-permute-start.5) | collective-permute-done | bytes 262176 | tf_op jit(solution)/shard_map/ppermute | solution.py:25
  138.1 2.7 convolution_bitcast_fusion
  146.1 40.2 %reduce-scatter.2.cloned.1.call-done = f32[512,256]{0,1:T(8,128)} async-done(((f32[4096,256]{0,1:T(8,128)}), f32[512,256]{0,1:T(8,128)}) %reduce-scatter.2.cloned.1.call-update) | async-done | bytes 524304 | tf_op jit(solution)/shard_map/reduce_scatter | solution.py:224
  187.6 2.2 fusion.36
  189.8 13.0 %all-reduce.1 = (f32[256]{0:T(256)S(1)}, f32[256]{0:T(256)S(1)}) all-reduce(f32[256]{0:T(256)S(1)} %get-tuple-element.143, f32[256]{0:T(256)S(1)} %get-tuple-element.142), channel_id=1, replica_groups=mesh['ctx'=64,'head'=8] {'head'}, use_global_device_ids=true, to_apply=%region_14.15 | all-reduce | flops 512 | bytes 4096 | tf_op jit(solution)/shard_map/psum | solution.py:63
  204.2 5.3 stack.33
  209.5 16.0 %all-to-all-start = ((bf16[64,1,4,128,128]{4,3,2,1,0:T(8,128)(2,1)}), bf16[64,1,4,128,128]{4,3,2,1,0:T(8,128)(2,1)}, u32[]{:S(2)}, u32[]{:S(2)}) async-start(bf16[64,1,4,128,128]{4,3,2,1,0:T(8,128)(2,1)} %stack.33), calls=%async_computation.1 | async-start | bytes 16777216 | tf_op jit(solution)/shard_map/all_to_all | solution.py:18
  235.2 357.6 %all-to-all-done = bf16[64,1,4,128,128]{4,3,2,1,0:T(8,128)(2,1)} async-done(((bf16[64,1,4,128,128]{4,3,2,1,0:T(8,128)(2,1)}), bf16[64,1,4,128,128]{4,3,2,1,0:T(8,128)(2,1)}, u32[]{:S(2)}, u32[]{:S(2)}) %all-to-all-start) | async-done | bytes 8388640 | tf_op jit(solution)/shard_map/all_to_all | solution.py:18
  592.8 11.5 %fusion.19 = bf16[4,1,128,128]{3,1,2,0:T(2,128)(2,1)S(1)} fusion(f32[4,64,1,1]{1,2,3,0:T(1,128)S(1)} %bitcast.264, bf16[64,4,128,128]{3,2,1,0:T(8,128)(2,1)} %bitcast.33), kind=kOutput, calls=%fused_computation.26 | convolution fusion | flops 50331648 | bytes 8520704 | tf_op jit(solution)/shard_map/hn,nhde->hde/dot_general | solution.py:97
  (194 shorter events, 60.6 us)
Async XLA Ops:
  7.2 131.0 %copy-start = (bf16[2,4096,128]{2,1,0:T(8,128)(2,1)S(1)}, bf16[2,4096,128]{2,1,0:T(8,128)(2,1)}, u32[]{:S(2)}) copy-start(bf16[2,4096,128]{2,1,0:T(8,128)(2,1)} %param.26) | copy-start | bytes 6291460
  7.2 27.4 %copy-start.22 = (bf16[256,128]{1,0:T(8,128)(2,1)S(1)}, bf16[256,128]{1,0:T(8,128)(2,1)}, u32[]{:S(2)}) copy-start(bf16[256,128]{1,0:T(8,128)(2,1)} %param.23) | copy-start | bytes 196612
  7.2 27.4 %copy-start.21 = (bf16[256,128]{1,0:T(8,128)(2,1)S(1)}, bf16[256,128]{1,0:T(8,128)(2,1)}, u32[]{:S(2)}) copy-start(bf16[256,128]{1,0:T(8,128)(2,1)} %param.24) | copy-start | bytes 196612
  7.2 179.0 %reduce-scatter.2.cloned.1.call-start = ((), (), s32[]{:S(2)}) async-start(), calls=%async_computation.2 | async-start | bytes 4718592 | tf_op jit(solution)/shard_map/reduce_scatter | solution.py:224
  8.3 22.9 %collective-permute-start = (bf16[2,256,128]{2,1,0:T(8,128)(2,1)S(1)}, bf16[2,256,128]{2,1,0:T(8,128)(2,1)S(1)}, u32[]{:S(2)}, u32[]{:S(2)}) collective-permute-start(bf16[2,256,128]{2,1,0:T(8,128)(2,1)S(1)} %pad_maximum_fusion.1), channel_id=1, source_target_pairs={{0,24},{8,32},{16,40},{24,48},{32,56},{40,64},{48,72},{56,80},{64,... | collective-permute-start | bytes 393224 | tf_op jit(solution)/shard_map/ppermute | solution.py:25
  16.0 15.2 %collective-permute-start.1 = (bf16[2,256,128]{2,1,0:T(8,128)(2,1)S(1)}, bf16[2,256,128]{2,1,0:T(8,128)(2,1)}, u32[]{:S(2)}, u32[]{:S(2)}) collective-permute-start(bf16[2,256,128]{2,1,0:T(8,128)(2,1)S(1)} %pad_maximum_fusion.1), channel_id=1, source_target_pairs={{0,16},{8,24},{16,32},{24,40},{32,48},{40,56},{48,64},{56,72},{64,... | collective-permute-start | bytes 393224 | tf_op jit(solution)/shard_map/ppermute | solution.py:25
  21.9 12.7 %collective-permute-start.2 = (bf16[2,256,128]{2,1,0:T(8,128)(2,1)S(1)}, bf16[2,256,128]{2,1,0:T(8,128)(2,1)}, u32[]{:S(2)}, u32[]{:S(2)}) collective-permute-start(bf16[2,256,128]{2,1,0:T(8,128)(2,1)S(1)} %pad_maximum_fusion.1), channel_id=1, source_target_pairs={{0,8},{8,16},{16,24},{24,32},{32,40},{40,48},{48,56},{56,64},{64,7... | collective-permute-start | bytes 393224 | tf_op jit(solution)/shard_map/ppermute | solution.py:25
  35.6 4.6 copy-start.3
  35.6 4.6 copy-start.5
  43.9 4.4 copy-start.2
  49.6 4.6 copy-start.3
  49.6 4.6 copy-start.5
  57.9 4.6 copy-start.2
  64.9 4.6 copy-start.3
  64.9 4.6 copy-start.5
  73.2 4.6 copy-start.2
  80.3 4.6 copy-start.3
  80.3 4.6 copy-start.5
  88.6 4.6 copy-start.2
  95.6 40.9 %copy-start.7 = (f32[1024,128]{1,0:T(8,128)S(1)}, f32[1024,128]{1,0:T(8,128)}, u32[]{:S(2)}) copy-start(f32[1024,128]{1,0:T(8,128)} %get-tuple-element.55) | copy-start | bytes 1572868
  96.9 15.5 %collective-permute-start.3 = (f32[2,256,128]{2,1,0:T(8,128)S(1)}, f32[2,256,128]{2,1,0:T(8,128)S(1)}, u32[]{:S(2)}, u32[]{:S(2)}) collective-permute-start(f32[2,256,128]{2,1,0:T(8,128)S(1)} %get-tuple-element.166), channel_id=1, source_target_pairs={{8,0},{16,8},{24,16},{32,24},{40,32},{48,40},{56,48},{64,56},{72,6... | collective-permute-start | bytes 786440 | tf_op jit(solution)/shard_map/ppermute | solution.py:25
  98.8 17.0 %collective-permute-start.4 = (f32[2,256,128]{2,1,0:T(8,128)S(1)}, f32[2,256,128]{2,1,0:T(8,128)S(1)}, u32[]{:S(2)}, u32[]{:S(2)}) collective-permute-start(f32[2,256,128]{2,1,0:T(8,128)S(1)} %get-tuple-element.168), channel_id=1, source_target_pairs={{16,0},{24,8},{32,16},{40,24},{48,32},{56,40},{64,48},{72,56},{80,... | collective-permute-start | bytes 786440 | tf_op jit(solution)/shard_map/ppermute | solution.py:25
  100.1 36.3 %collective-permute-start.5 = (f32[2,256,128]{2,1,0:T(8,128)S(1)}, f32[2,256,128]{2,1,0:T(8,128)S(1)}, u32[]{:S(2)}, u32[]{:S(2)}) collective-permute-start(f32[2,256,128]{2,1,0:T(8,128)S(1)} %get-tuple-element.167), channel_id=1, source_target_pairs={{24,0},{32,8},{40,16},{48,24},{56,32},{64,40},{72,48},{80,56},{88,... | collective-permute-start | bytes 786440 | tf_op jit(solution)/shard_map/ppermute | solution.py:25
  140.8 2.9 copy-start.14
  140.8 4.1 copy-start.16
  144.9 42.7 %copy-start.19 = (bf16[1,4,128,128]{3,2,1,0:T(8,128)(2,1)S(1)}, bf16[1,4,128,128]{3,2,1,0:T(8,128)(2,1)}, u32[]{:S(2)}) copy-start(bf16[1,4,128,128]{3,2,1,0:T(8,128)(2,1)} %param.21) | copy-start | bytes 393220
  144.9 42.7 %copy-start.26 = (f32[512]{0:T(512)S(1)}, f32[512]{0:T(512)}, u32[]{:S(2)}) copy-start(f32[512]{0:T(512)} %param.19) | copy-start | bytes 6148
  209.5 19.5 %copy-start.18 = (bf16[4,512,128]{2,1,0:T(8,128)(2,1)S(1)}, bf16[4,512,128]{2,1,0:T(8,128)(2,1)}, u32[]{:S(2)}) copy-start(bf16[4,512,128]{2,1,0:T(8,128)(2,1)} %get-tuple-element.57) | copy-start | bytes 1572868
  209.5 383.3 %all-to-all-start = ((bf16[64,1,4,128,128]{4,3,2,1,0:T(8,128)(2,1)}), bf16[64,1,4,128,128]{4,3,2,1,0:T(8,128)(2,1)}, u32[]{:S(2)}, u32[]{:S(2)}) async-start(bf16[64,1,4,128,128]{4,3,2,1,0:T(8,128)(2,1)} %stack.33), calls=%async_computation.1 | async-start | bytes 16777216 | tf_op jit(solution)/shard_map/all_to_all | solution.py:18
  225.5 4.7 copy-start.17
  231.8 361.0 %copy-start.25 = (f32[4,64]{1,0:T(4,128)S(1)}, f32[4,64]{1,0:T(4,128)}, u32[]{:S(2)}) copy-start(f32[4,64]{1,0:T(4,128)} %exponential_select_fusion.1) | copy-start | bytes 3076
  592.8 11.7 %copy-start.12 = (f32[256,4,128]{0,2,1:T(8,128)S(1)}, f32[256,4,128]{0,2,1:T(8,128)}, u32[]{:S(2)}) copy-start(f32[256,4,128]{0,2,1:T(8,128)} %convolution_bitcast_fusion.4) | copy-start | bytes 1572868
  (27 other events, 54.6 us)
Sparse Core Ops, SparseCore 0:
  141.0 45.2 reduce-scatter.1
